TPU v7x, 32 devices: a whole 2x2x4 slice. The times are simulated.
32 devices in a mesh: clip: 2 (over y), pos: 16 (over z, x, core).
Axes of the slice: x: 2, y: 2, z: 4, core: 2. Of those that a mesh axis runs over, the one named last changes fastest.
Arguments:
- tokens: bfloat16 [128, 256, 768], P('clip', 'pos'), may hold values from -6 to 6
- clip_lengths: int32 [2, 4], P('clip'), may hold values from 1 to 32, 64 in all within a row
- timesteps: int32 [2, 4], P('clip'), may hold values from 0 to 999
- embed_first: bfloat16 [256, 768], replicated, may hold values from -0.375 to 0.375
- embed_second: bfloat16 [768, 768], replicated, may hold values from -0.21875 to 0.21875
- adaln_weight: bfloat16 [768, 6912], replicated, may hold values from -0.4375 to 0.4375
- spatial_in: bfloat16 [768, 2304], replicated, may hold values from -0.21875 to 0.21875
- spatial_out: bfloat16 [768, 768], replicated, may hold values from -0.875 to 0.875
- temporal_in: bfloat16 [768, 2304], replicated, may hold values from -0.21875 to 0.21875
- temporal_out: bfloat16 [768, 768], replicated, may hold values from -0.4375 to 0.4375
- hidden_up: bfloat16 [768, 3072], replicated, may hold values from -0.21875 to 0.21875
- hidden_down: bfloat16 [3072, 768], replicated, may hold values from -0.109375 to 0.109375
- grad_output: bfloat16 [128, 256, 768], P('clip', 'pos'), may hold values from -6 to 6
Outputs:
- block_out: bfloat16 [128, 256, 768], P('clip', 'pos')
- grad_tokens: bfloat16 [128, 256, 768], P('clip', 'pos')
- grad_embed_first: float32 [256, 768], P('pos')
- grad_embed_second: float32 [768, 768], P('pos')
- grad_adaln_weight: float32 [768, 6912], P('pos')
- grad_spatial_in: float32 [768, 2304], P('pos')
- grad_spatial_out: float32 [768, 768], P('pos')
- grad_temporal_in: float32 [768, 2304], P('pos')
- grad_temporal_out: float32 [768, 768], P('pos')
- grad_hidden_up: float32 [768, 3072], P('pos')
- grad_hidden_down: float32 [3072, 768], P('pos')
Inputs may be any that keep to these rules, and one draw needn't show every extreme that they name: `clip_lengths`: row r lists in order the frame counts of the 4 clips that fill frames r * 64 to (r + 1) * 64 - 1; every row sums to 64 and its longest clip has 32 frames. `timesteps`: one diffusion timestep index per clip, in the order of clip_lengths.
All inputs are finite; a program needn't handle non-finite values.
Results may differ from a plain program's by a relative error of at most 0.02.
Values may be sent and summed in bfloat16 or wider, within the bound.
A program may use at most 448 MiB of HBM per device.

v0:
```python
from functools import partial
import math
import jax
import jax.numpy as jnp
from jax import lax
from jax.sharding import PartitionSpec as P

HEADS = 12
HEAD_DIM = 64
FREQ = 256
epsilon = 1e-06
highest = lax.Precision.HIGHEST
masked_score = -1000000000.0


def frequency(step_ids):
    half_width = FREQ // 2
    rate_table = jnp.exp(
        -math.log(10000.0) * jnp.arange(half_width, dtype=jnp.float32) / half_width
    )
    angles = step_ids.astype(jnp.float32)[:, None] * rate_table[None, :]
    return jnp.concatenate([jnp.cos(angles), jnp.sin(angles)], axis=1)


def modulation(step_ids, first_w, second_w, adaln_w):
    hidden_cond = jax.nn.silu(
        jnp.dot(frequency(step_ids), first_w, precision=highest, preferred_element_type=jnp.float32)
    )
    cond_vec = jnp.dot(hidden_cond, second_w, precision=highest, preferred_element_type=jnp.float32)
    return jnp.dot(
        jax.nn.silu(cond_vec), adaln_w, precision=highest, preferred_element_type=jnp.float32
    )


def clip_onehot(lengths, frames):
    clip_ends = jnp.cumsum(lengths)
    frame_ids = jnp.arange(frames, dtype=jnp.int32)
    clip_ids = jnp.sum((frame_ids[:, None] >= clip_ends[None, :]).astype(jnp.int32), axis=1)
    onehot = (clip_ids[:, None] == jnp.arange(lengths.shape[0], dtype=jnp.int32)[None, :]).astype(
        jnp.float32
    )
    return (onehot, clip_ids)


def norm_mod(values, shift_vec, scale_vec):
    centre = values - jnp.mean(values, axis=-1, keepdims=True)
    spread = jnp.mean(centre * centre, axis=-1, keepdims=True)
    return centre * lax.rsqrt(spread + epsilon) * (1.0 + scale_vec) + shift_vec


def gelu_tanh(values):
    return jax.nn.gelu(values, approximate=True)


def project(normed, weight):
    frames, places, model_width = normed.shape
    joined = jnp.dot(
        normed.reshape(frames * places, model_width), weight, preferred_element_type=jnp.float32
    )
    return joined.astype(jnp.bfloat16).reshape(frames, places, 3, HEADS, HEAD_DIM)


def weight_grad(left, right):
    return jnp.einsum("rd,rk->dk", left, right, preferred_element_type=jnp.float32)


def input_grad(grad_rows, weight):
    return jnp.einsum("rk,dk->rd", grad_rows, weight, preferred_element_type=jnp.float32)


def score_block(query_heads, key_heads, factor):
    return (
        jnp.einsum("fqhd,fkhd->fhqk", query_heads, key_heads, preferred_element_type=jnp.float32)
        * factor
    )


def on_device(
    tokens,
    clip_lengths,
    timesteps,
    embed_first,
    embed_second,
    adaln_weight,
    spatial_in,
    spatial_out,
    temporal_in,
    temporal_out,
    hidden_up,
    hidden_down,
    grad_output,
):
    frames, places, model_width = tokens.shape
    row_count = frames * places
    factor = 1.0 / math.sqrt(HEAD_DIM)
    modulated, cond_pull = jax.vjp(
        partial(modulation, timesteps[0]),
        embed_first.astype(jnp.float32),
        embed_second.astype(jnp.float32),
        adaln_weight.astype(jnp.float32),
    )
    onehot, clip_ids = clip_onehot(clip_lengths[0], frames)
    per_frame = jnp.einsum(
        "fc,cm->fm", onehot, modulated, precision=highest, preferred_element_type=jnp.float32
    )
    pieces = [
        per_frame[:, None, slot_index * model_width : (slot_index + 1) * model_width]
        for slot_index in range(9)
    ]
    token_x = tokens.astype(jnp.float32)
    normed_one, norm_pull_one = jax.vjp(norm_mod, token_x, pieces[0], pieces[1])
    h_one = normed_one.astype(jnp.bfloat16)
    qkv_one = project(h_one, spatial_in)
    q_space = qkv_one[:, :, 0]
    k_local = qkv_one[:, :, 1].reshape(frames, places, model_width)
    v_local = qkv_one[:, :, 2].reshape(frames, places, model_width)
    k_all, v_all = (
        lax.all_gather(k_local, "pos", axis=1, tiled=True),
        lax.all_gather(v_local, "pos", axis=1, tiled=True),
    )
    patch_count = k_all.shape[1]
    k_heads = k_all.reshape(frames, patch_count, HEADS, HEAD_DIM)
    v_heads = v_all.reshape(frames, patch_count, HEADS, HEAD_DIM)
    space_scores = score_block(q_space, k_heads, factor)
    space_top = jnp.max(space_scores, axis=-1, keepdims=True)
    space_lse = space_top + jnp.log(
        jnp.sum(jnp.exp(space_scores - space_top), axis=-1, keepdims=True)
    )
    space_probs = jnp.exp(space_scores - space_lse).astype(jnp.bfloat16)
    o_one = jnp.einsum("fhqk,fkhd->fqhd", space_probs, v_heads, preferred_element_type=jnp.float32)
    o_one = o_one.astype(jnp.bfloat16).reshape(row_count, model_width)
    y_one = jnp.dot(o_one, spatial_out, preferred_element_type=jnp.float32).reshape(
        frames, places, model_width
    )
    x_one = token_x + pieces[2] * y_one
    normed_two, norm_pull_two = jax.vjp(norm_mod, x_one, pieces[3], pieces[4])
    h_two = normed_two.astype(jnp.bfloat16)
    qkv_two = project(h_two, temporal_in)
    q_time = qkv_two[:, :, 0]
    k_time = qkv_two[:, :, 1]
    v_time = qkv_two[:, :, 2]
    same_clip = (clip_ids[:, None] == clip_ids[None, :])[None, None]
    time_scores = (
        jnp.einsum("fphd,gphd->phfg", q_time, k_time, preferred_element_type=jnp.float32) * factor
    )
    time_scores = jnp.where(same_clip, time_scores, masked_score)
    time_top = jnp.max(time_scores, axis=-1, keepdims=True)
    time_lse = time_top + jnp.log(jnp.sum(jnp.exp(time_scores - time_top), axis=-1, keepdims=True))
    time_probs = jnp.exp(time_scores - time_lse)
    time_low = time_probs.astype(jnp.bfloat16)
    o_two = jnp.einsum("phfg,gphd->fphd", time_low, v_time, preferred_element_type=jnp.float32)
    o_two = o_two.astype(jnp.bfloat16).reshape(row_count, model_width)
    y_two = jnp.dot(o_two, temporal_out, preferred_element_type=jnp.float32).reshape(
        frames, places, model_width
    )
    x_two = x_one + pieces[5] * y_two
    normed_three, norm_pull_three = jax.vjp(norm_mod, x_two, pieces[6], pieces[7])
    h_three = normed_three.astype(jnp.bfloat16).reshape(row_count, model_width)
    upward = jnp.dot(h_three, hidden_up, preferred_element_type=jnp.float32)
    activated, gelu_pull = jax.vjp(gelu_tanh, upward)
    act_low = activated.astype(jnp.bfloat16)
    z_out = jnp.dot(act_low, hidden_down, preferred_element_type=jnp.float32).reshape(
        frames, places, model_width
    )
    block_out = (x_two + pieces[8] * z_out).astype(jnp.bfloat16)
    grad_top = grad_output.astype(jnp.float32)
    grad_gate_three = jnp.sum(grad_top * z_out, axis=1)
    grad_z = (pieces[8] * grad_top).astype(jnp.bfloat16).reshape(row_count, model_width)
    grad_hidden_down = weight_grad(act_low, grad_z)
    grad_act = input_grad(grad_z, hidden_down)
    grad_up_rows = gelu_pull(grad_act)[0].astype(jnp.bfloat16)
    grad_hidden_up = weight_grad(h_three, grad_up_rows)
    grad_h_three = input_grad(grad_up_rows, hidden_up).reshape(frames, places, model_width)
    grad_norm_three, grad_shift_three, grad_scale_three = norm_pull_three(grad_h_three)
    grad_two = grad_top + grad_norm_three
    grad_gate_two = jnp.sum(grad_two * y_two, axis=1)
    grad_y_two = (pieces[5] * grad_two).astype(jnp.bfloat16).reshape(row_count, model_width)
    grad_temporal_out = weight_grad(o_two, grad_y_two)
    grad_o_two = (
        input_grad(grad_y_two, temporal_out)
        .astype(jnp.bfloat16)
        .reshape(frames, places, HEADS, HEAD_DIM)
    )
    grad_time_probs = jnp.einsum(
        "fphd,gphd->phfg", grad_o_two, v_time, preferred_element_type=jnp.float32
    )
    time_inner = jnp.sum(grad_time_probs * time_probs, axis=-1, keepdims=True)
    grad_time_scores = (time_probs * (grad_time_probs - time_inner)).astype(jnp.bfloat16)
    grad_q_time = (
        jnp.einsum("phfg,gphd->fphd", grad_time_scores, k_time, preferred_element_type=jnp.float32)
        * factor
    )
    grad_k_time = (
        jnp.einsum("phfg,fphd->gphd", grad_time_scores, q_time, preferred_element_type=jnp.float32)
        * factor
    )
    grad_v_time = jnp.einsum(
        "phfg,fphd->gphd", time_low, grad_o_two, preferred_element_type=jnp.float32
    )
    grad_qkv_two = (
        jnp.stack([grad_q_time, grad_k_time, grad_v_time], axis=2)
        .astype(jnp.bfloat16)
        .reshape(row_count, 3 * model_width)
    )
    grad_temporal_in = weight_grad(h_two.reshape(row_count, model_width), grad_qkv_two)
    grad_h_two = input_grad(grad_qkv_two, temporal_in).reshape(frames, places, model_width)
    grad_norm_two, grad_shift_two, grad_scale_two = norm_pull_two(grad_h_two)
    grad_one = grad_two + grad_norm_two
    grad_gate_one = jnp.sum(grad_one * y_one, axis=1)
    grad_y_one = (pieces[2] * grad_one).astype(jnp.bfloat16).reshape(row_count, model_width)
    grad_spatial_out = weight_grad(o_one, grad_y_one)
    grad_o_one = (
        input_grad(grad_y_one, spatial_out)
        .astype(jnp.bfloat16)
        .reshape(frames, places, model_width)
    )
    k_back, v_back = (k_all, v_all)
    k_back_heads = k_back.reshape(frames, patch_count, HEADS, HEAD_DIM)
    v_back_heads = v_back.reshape(frames, patch_count, HEADS, HEAD_DIM)
    grad_o_heads = grad_o_one.reshape(frames, places, HEADS, HEAD_DIM)
    again_probs = jnp.exp(score_block(q_space, k_back_heads, factor) - space_lse)
    grad_space_probs = jnp.einsum(
        "fqhd,fkhd->fhqk", grad_o_heads, v_back_heads, preferred_element_type=jnp.float32
    )
    space_inner = jnp.sum(grad_space_probs * again_probs, axis=-1, keepdims=True)
    grad_space_scores = (again_probs * (grad_space_probs - space_inner)).astype(jnp.bfloat16)
    grad_q_space = (
        jnp.einsum(
            "fhqk,fkhd->fqhd", grad_space_scores, k_back_heads, preferred_element_type=jnp.float32
        )
        * factor
    )
    key_terms = (
        jnp.einsum(
            "fhqk,fqhd->fkhd", grad_space_scores, q_space, preferred_element_type=jnp.float32
        )
        * factor
    )
    value_terms = jnp.einsum(
        "fhqk,fqhd->fkhd",
        again_probs.astype(jnp.bfloat16),
        grad_o_heads,
        preferred_element_type=jnp.float32,
    )
    grad_keys, grad_values = (
        lax.psum_scatter(
            key_terms.reshape(frames, patch_count, model_width).astype(jnp.bfloat16),
            "pos",
            scatter_dimension=1,
            tiled=True,
        ).astype(jnp.float32),
        lax.psum_scatter(
            value_terms.reshape(frames, patch_count, model_width).astype(jnp.bfloat16),
            "pos",
            scatter_dimension=1,
            tiled=True,
        ).astype(jnp.float32),
    )
    grad_qkv_one = jnp.stack(
        [grad_q_space.reshape(frames, places, model_width), grad_keys, grad_values], axis=2
    )
    grad_qkv_one = grad_qkv_one.astype(jnp.bfloat16).reshape(row_count, 3 * model_width)
    grad_spatial_in = weight_grad(h_one.reshape(row_count, model_width), grad_qkv_one)
    grad_h_one = input_grad(grad_qkv_one, spatial_in).reshape(frames, places, model_width)
    grad_norm_one, grad_shift_one, grad_scale_one = norm_pull_one(grad_h_one)
    grad_tokens = (grad_one + grad_norm_one).astype(jnp.bfloat16)
    grad_frames = jnp.concatenate(
        [
            grad_shift_one[:, 0],
            grad_scale_one[:, 0],
            grad_gate_one,
            grad_shift_two[:, 0],
            grad_scale_two[:, 0],
            grad_gate_two,
            grad_shift_three[:, 0],
            grad_scale_three[:, 0],
            grad_gate_three,
        ],
        axis=1,
    )
    grad_modulation = jnp.einsum(
        "fc,fm->cm", onehot, grad_frames, precision=highest, preferred_element_type=jnp.float32
    )
    grad_embed_first, grad_embed_second, grad_adaln_weight = cond_pull(grad_modulation)
    summed = (
        lax.psum_scatter(
            grad_embed_first.astype(jnp.bfloat16), "pos", scatter_dimension=0, tiled=True
        ).astype(jnp.float32),
        lax.psum_scatter(
            grad_embed_second.astype(jnp.bfloat16), "pos", scatter_dimension=0, tiled=True
        ).astype(jnp.float32),
        lax.psum_scatter(
            grad_adaln_weight.astype(jnp.bfloat16), "pos", scatter_dimension=0, tiled=True
        ).astype(jnp.float32),
        lax.psum_scatter(
            grad_spatial_in.astype(jnp.bfloat16), "pos", scatter_dimension=0, tiled=True
        ).astype(jnp.float32),
        lax.psum_scatter(
            grad_spatial_out.astype(jnp.bfloat16), "pos", scatter_dimension=0, tiled=True
        ).astype(jnp.float32),
        lax.psum_scatter(
            grad_temporal_in.astype(jnp.bfloat16), "pos", scatter_dimension=0, tiled=True
        ).astype(jnp.float32),
        lax.psum_scatter(
            grad_temporal_out.astype(jnp.bfloat16), "pos", scatter_dimension=0, tiled=True
        ).astype(jnp.float32),
        lax.psum_scatter(
            grad_hidden_up.astype(jnp.bfloat16), "pos", scatter_dimension=0, tiled=True
        ).astype(jnp.float32),
        lax.psum_scatter(
            grad_hidden_down.astype(jnp.bfloat16), "pos", scatter_dimension=0, tiled=True
        ).astype(jnp.float32),
    )
    summed = (
        lax.psum(summed[0].astype(jnp.bfloat16), "clip").astype(jnp.float32),
        lax.psum(summed[1].astype(jnp.bfloat16), "clip").astype(jnp.float32),
        lax.psum(summed[2].astype(jnp.bfloat16), "clip").astype(jnp.float32),
        lax.psum(summed[3].astype(jnp.bfloat16), "clip").astype(jnp.float32),
        lax.psum(summed[4].astype(jnp.bfloat16), "clip").astype(jnp.float32),
        lax.psum(summed[5].astype(jnp.bfloat16), "clip").astype(jnp.float32),
        lax.psum(summed[6].astype(jnp.bfloat16), "clip").astype(jnp.float32),
        lax.psum(summed[7].astype(jnp.bfloat16), "clip").astype(jnp.float32),
        lax.psum(summed[8].astype(jnp.bfloat16), "clip").astype(jnp.float32),
    )
    return (
        block_out,
        grad_tokens,
        summed[0],
        summed[1],
        summed[2],
        summed[3],
        summed[4],
        summed[5],
        summed[6],
        summed[7],
        summed[8],
    )


def solution(mesh):
    in_specs = (
        P("clip", "pos", None),
        P("clip", None),
        P("clip", None),
        P(),
        P(),
        P(),
        P(),
        P(),
        P(),
        P(),
        P(),
        P(),
        P("clip", "pos", None),
    )
    out_specs = (
        P("clip", "pos", None),
        P("clip", "pos", None),
        P("pos", None),
        P("pos", None),
        P("pos", None),
        P("pos", None),
        P("pos", None),
        P("pos", None),
        P("pos", None),
        P("pos", None),
        P("pos", None),
    )
    return jax.shard_map(
        on_device, mesh=mesh, in_specs=in_specs, out_specs=out_specs, check_vma=False
    )
```

profile of v0, /device:TPU:0, one launch (start us, length us, event | category | flops | bytes accessed | tf_op | source)
XLA Modules:
  0.0 1902.6 jit_solution(2923653464098898793)
XLA Ops:
  14.0 7.0 fusion.78
  26.3 5.4 convolution_convert_fusion.3
  31.7 15.0 reshape.275
  46.7 9.2 fusion.90
  55.9 6.1 reshape_squeeze.7
  62.1 6.1 reshape_squeeze.6
  68.8 124.6 %all-gather.5.cloned.1.call-done = bf16[64,256,768]{2,1,0:T(8,128)(2,1)} async-done(((bf16[64,16,768]{2,1,0:T(8,128)(2,1)}), bf16[64,256,768]{2,1,0:T(8,128)(2,1)}) %all-gather.5.cloned.1.call-update) | async-done | bytes 25165840 | tf_op jit(solution)/shard_map/all_gather | solution.py:118
  193.5 30.7 %copy.79 = bf16[64,256,768]{1,2,0:T(8,128)(2,1)} copy(bf16[64,256,768]{2,1,0:T(8,128)(2,1)} %all-gather.5.cloned.1.call-done) | data formatting | bytes 50331648 | tf_op jit(solution)/shard_map/all_gather | solution.py:118
  224.2 18.9 multiply_reduce_fusion.1
  243.1 8.6 exponential_reduce_fusion
  252.7 71.5 %all-gather.3.cloned.1.call-done = bf16[64,256,768]{2,1,0:T(8,128)(2,1)} async-done(((bf16[64,16,768]{2,1,0:T(8,128)(2,1)}), bf16[64,256,768]{2,1,0:T(8,128)(2,1)}) %all-gather.3.cloned.1.call-update) | async-done | bytes 25165840 | tf_op jit(solution)/shard_map/all_gather | solution.py:119
  324.1 31.5 %copy.77 = bf16[64,256,768]{1,2,0:T(8,128)(2,1)} copy(bf16[64,256,768]{2,1,0:T(8,128)(2,1)} %all-gather.3.cloned.1.call-done) | data formatting | bytes 50331648 | tf_op jit(solution)/shard_map/all_gather | solution.py:119
  355.6 16.2 convert_bitcast_fusion
  376.8 6.1 dot_general.132
  382.9 5.4 fusion.88
  391.6 5.4 convolution_convert_fusion.2
  397.0 15.0 reshape.279
  412.0 9.2 fusion.89
  421.2 6.7 copy.119
  427.9 8.2 fusion.8
  448.5 5.8 fusion.87
  457.2 7.1 fusion.93
  464.3 7.3 fusion.86
  471.7 16.5 fusion.6
  488.2 9.0 fusion.94
  513.2 5.9 reshape.285
  519.1 6.5 copy.94
  525.6 7.4 convolution_bitcast_fusion
  533.1 8.0 multiply_reduce_fusion.2
  555.7 9.6 maximum_convert_fusion
  565.3 12.3 copy.97
  577.6 15.8 convert_element_type.240
  593.5 7.5 multiply_reduce_fusion.6
  616.8 17.5 convolution_convert_fusion
  634.3 32.6 %copy.102 = bf16[64,256,768]{2,1,0:T(8,128)(2,1)} copy(bf16[64,256,768]{1,2,0:T(8,128)(2,1)} %bitcast.161) | data formatting | bytes 50331648 | tf_op jit(solution)/shard_map/convert_element_type | solution.py:253
  667.0 26.9 %multiply_reduce_fusion = (f32[64,12,16]{2,1,0:T(8,128)S(1)}, f32[64,12,16,256]{3,2,1,0:T(8,128)}) fusion(f32[64,12,16,256]{3,2,1,0:T(8,128)} %get-tuple-element.58, f32[64,12,16]{2,1,0:T(8,128)S(1)} %copy-done.14, bf16[64,256,12,64]{1,3,2,0:T(8,128)(2,1)} %bitcast.156, bf16[64,16,12,64]{3,2,1,0:T(8,128)(2,1)} %reshape_reshape.3), kind=kOutput, calls=%fused_computation.13 | convolution fusion | flops 415223808 | bytes 52002816 | tf_op jit(solution)/shard_map/fqhd,fkhd->fhqk/dot_general | solution.py:222
  693.9 12.4 multiply_convert_fusion.1
  706.3 14.0 multiply_convert_fusion
  720.3 30.1 %copy.100 = bf16[64,256,768]{2,1,0:T(8,128)(2,1)} copy(bf16[64,256,768]{1,2,0:T(8,128)(2,1)} %bitcast.162) | data formatting | bytes 50331648 | tf_op jit(solution)/shard_map/convert_element_type | solution.py:247
  752.3 6.0 copy.107
  758.3 5.4 reshape.288
  766.3 5.3 reshape.287
  774.2 16.0 convert_element_type.264
  790.1 7.8 convolution_convert_fusion.6
  799.3 11.6 convolution_convert_fusion.4
  812.3 9.6 convolution_convert_fusion.5
  821.9 13.6 multiply_bitcast_fusion
  838.6 5.2 stack_reshape.3
  843.8 66.5 %reduce-scatter.14.cloned.1.call-done = bf16[64,16,768]{2,1,0:T(8,128)(2,1)} async-done(((bf16[64,256,768]{2,1,0:T(8,128)(2,1)}), bf16[64,16,768]{2,1,0:T(8,128)(2,1)}) %reduce-scatter.14.cloned.1.call-update) | async-done | bytes 1572880 | tf_op jit(solution)/shard_map/reduce_scatter | solution.py:252
  910.4 246.4 %reduce-scatter.12.cloned.1.call-done = bf16[64,16,768]{2,1,0:T(8,128)(2,1)} async-done(((bf16[64,256,768]{2,1,0:T(8,128)(2,1)}), bf16[64,16,768]{2,1,0:T(8,128)(2,1)}) %reduce-scatter.12.cloned.1.call-update) | async-done | bytes 1572880 | tf_op jit(solution)/shard_map/reduce_scatter | solution.py:246
  1169.7 8.3 fusion.95
  1185.3 6.5 copy.103
  1193.2 5.3 convolution_convert_fusion.7
  1198.6 19.3 %convolution_convert_fusion.1 = bf16[768,6912]{1,0:T(8,128)(2,1)} fusion(f32[4,6912]{1,0:T(4,128)S(1)} %fusion.48, f32[4,768]{1,0:T(4,128)S(1)} %copy-done.71), kind=kOutput, calls=%fused_computation.17 | convolution fusion | flops 260124672 | bytes 10739712 | tf_op jit(solution)/shard_map/transpose(jvp())/dot_general | solution.py:30
  1221.9 56.2 %reduce-scatter.24.cloned.1.call-done = bf16[48,768]{1,0:T(8,128)(2,1)} async-done(((bf16[768,768]{1,0:T(8,128)(2,1)}), bf16[48,768]{1,0:T(8,128)(2,1)}) %reduce-scatter.24.cloned.1.call-update) | async-done | bytes 73744 | tf_op jit(solution)/shard_map/reduce_scatter | solution.py:298
  1278.2 71.0 %reduce-scatter.26.cloned.1.call-done = bf16[48,2304]{1,0:T(8,128)(2,1)} async-done(((bf16[768,2304]{1,0:T(8,128)(2,1)}), bf16[48,2304]{1,0:T(8,128)(2,1)}) %reduce-scatter.26.cloned.1.call-update) | async-done | bytes 221200 | tf_op jit(solution)/shard_map/reduce_scatter | solution.py:301
  1349.2 78.5 %reduce-scatter.32.cloned.1.call-done = bf16[192,768]{1,0:T(8,128)(2,1)} async-done(((bf16[3072,768]{1,0:T(8,128)(2,1)}), bf16[192,768]{1,0:T(8,128)(2,1)}) %reduce-scatter.32.cloned.1.call-update) | async-done | bytes 294928 | tf_op jit(solution)/shard_map/reduce_scatter | solution.py:310
  1427.7 78.6 %reduce-scatter.30.cloned.1.call-done = bf16[48,3072]{1,0:T(8,128)(2,1)} async-done(((bf16[768,3072]{1,0:T(8,128)(2,1)}), bf16[48,3072]{1,0:T(8,128)(2,1)}) %reduce-scatter.30.cloned.1.call-update) | async-done | bytes 294928 | tf_op jit(solution)/shard_map/reduce_scatter | solution.py:307
  1506.3 61.5 %reduce-scatter.18.cloned.1.call-done = bf16[48,768]{1,0:T(8,128)(2,1)} async-done(((bf16[768,768]{1,0:T(8,128)(2,1)}), bf16[48,768]{1,0:T(8,128)(2,1)}) %reduce-scatter.18.cloned.1.call-update) | async-done | bytes 73744 | tf_op jit(solution)/shard_map/reduce_scatter | solution.py:289
  1567.8 71.0 %reduce-scatter.22.cloned.1.call-done = bf16[48,2304]{1,0:T(8,128)(2,1)} async-done(((bf16[768,2304]{1,0:T(8,128)(2,1)}), bf16[48,2304]{1,0:T(8,128)(2,1)}) %reduce-scatter.22.cloned.1.call-update) | async-done | bytes 221200 | tf_op jit(solution)/shard_map/reduce_scatter | solution.py:295
  1638.8 123.6 %reduce-scatter.20.cloned.1.call-done = bf16[48,6912]{1,0:T(8,128)(2,1)} async-done(((bf16[768,6912]{1,0:T(8,128)(2,1)}), bf16[48,6912]{1,0:T(8,128)(2,1)}) %reduce-scatter.20.cloned.1.call-update) | async-done | bytes 663568 | tf_op jit(solution)/shard_map/reduce_scatter | solution.py:292
  1767.5 54.7 %reduce-scatter.16.cloned.1.call-done = bf16[16,768]{1,0:T(8,128)(2,1)} async-done(((bf16[256,768]{1,0:T(8,128)(2,1)}), bf16[16,768]{1,0:T(8,128)(2,1)}) %reduce-scatter.16.cloned.1.call-update) | async-done | bytes 24592 | tf_op jit(solution)/shard_map/reduce_scatter | solution.py:286
  1822.2 9.5 psum.63
  1833.0 49.9 %all-reduce.3.cloned.1.call-done = (bf16[48,768]{1,0:T(8,128)(2,1)}, bf16[48,6912]{1,0:T(8,128)(2,1)}, bf16[48,2304]{1,0:T(8,128)(2,1)}, bf16[48,768]{1,0:T(8,12...) async-done(((bf16[48,768]{1,0:T(8,128)(2,1)}, bf16[48,6912]{1,0:T(8,128)(2,1)}, ...) | async-done | bytes 1916944 | tf_op jit(solution)/shard_map/psum | solution.py:316
  (310 shorter events, 140.6 us)
Async XLA Ops:
  7.2 384.4 %copy-start = (bf16[768,2304]{1,0:T(8,128)(2,1)S(1)}, bf16[768,2304]{1,0:T(8,128)(2,1)}, u32[]{:S(2)}) copy-start(bf16[768,2304]{1,0:T(8,128)(2,1)} %param.21) | copy-start | bytes 10616836
  7.2 186.3 %all-gather.5.cloned.1.call-start = ((), (), s32[]{:S(2)}) async-start(), calls=%async_computation.12 | async-start | bytes 26738688 | tf_op jit(solution)/shard_map/all_gather | solution.py:118
  8.2 4.7 copy-start.72
  8.2 5.2 copy-start.26
  8.3 60.4 %copy-start.87 = (s32[64]{0:T(128)}, s32[64]{0:T(128)S(1)}, u32[]{:S(2)}) copy-start(s32[64]{0:T(128)S(1)} %convert_reduce_fusion.1) | copy-start | bytes 772
  10.8 12.2 copy-start.54
  12.8 10.2 copy-start.66
  12.9 8.1 copy-start.83
  12.9 8.1 copy-start.85
  13.4 7.6 copy-start.80
  14.0 7.0 copy-start.70
  62.0 262.1 %all-gather.3.cloned.1.call-start = ((), (), s32[]{:S(2)}) async-start(), calls=%async_computation.11 | async-start | bytes 26738688 | tf_op jit(solution)/shard_map/all_gather | solution.py:119
  68.2 842.2 %reduce-scatter.14.cloned.1.call-start = ((), (), s32[]{:S(2)}) async-start(), calls=%async_computation.14 | async-start | bytes 26738688 | tf_op jit(solution)/shard_map/reduce_scatter | solution.py:252
  243.1 8.7 copy-start.25
  436.2 4.2 copy-start.11
  454.8 9.5 slice-start.5
  457.2 7.1 slice-start.6
  464.3 7.4 copy-start.91
  464.3 7.4 copy-start.40
  471.7 28.3 %copy-start.19 = (f32[1024,768]{1,0:T(8,128)}, f32[1024,768]{1,0:T(8,128)S(1)}, u32[]{:S(2)}) copy-start(f32[1024,768]{1,0:T(8,128)S(1)} %fusion.86) | copy-start | bytes 9437188
  506.3 4.3 copy-start.50
  525.6 7.5 copy-start.12
  525.6 7.5 copy-start.13
  525.6 7.5 copy-start.29
  525.6 15.5 slice-start
  533.1 8.0 slice-start.1
  541.1 4.5 copy-start.18
  545.6 5.2 copy-start.17
  593.4 7.6 copy-start.77
  593.5 7.6 copy-start.4
  593.5 7.6 copy-start.31
  593.5 7.6 copy-start.53
  593.5 7.6 copy-start.69
  593.5 10.5 copy-start.20
  593.5 10.5 copy-start.21
  593.5 10.5 copy-start.22
  604.0 5.8 copy-start.37
  608.2 3.3 copy-start.51
  613.0 3.9 copy-start.14
  666.9 489.8 %reduce-scatter.12.cloned.1.call-start = ((), (), s32[]{:S(2)}) async-start(), calls=%async_computation.13 | async-start | bytes 26738688 | tf_op jit(solution)/shard_map/reduce_scatter | solution.py:246
  706.3 14.0 copy-start.5
  750.4 471.5 %reduce-scatter.28.cloned.1.call-start = ((), (), s32[]{:S(2)}) async-start(), calls=%async_computation.21 | async-start | bytes 1253376 | tf_op jit(solution)/shard_map/reduce_scatter | solution.py:304
  758.3 5.4 copy-start.47
  766.2 5.4 copy-start.49
  766.2 512.0 %reduce-scatter.24.cloned.1.call-start = ((), (), s32[]{:S(2)}) async-start(), calls=%async_computation.19 | async-start | bytes 1253376 | tf_op jit(solution)/shard_map/reduce_scatter | solution.py:298
  774.1 16.0 copy-start.43
  774.1 575.1 %reduce-scatter.26.cloned.1.call-start = ((), (), s32[]{:S(2)}) async-start(), calls=%async_computation.20 | async-start | bytes 3760128 | tf_op jit(solution)/shard_map/reduce_scatter | solution.py:301
  797.9 629.7 %reduce-scatter.32.cloned.1.call-start = ((), (), s32[]{:S(2)}) async-start(), calls=%async_computation.23 | async-start | bytes 5013504 | tf_op jit(solution)/shard_map/reduce_scatter | solution.py:310
  810.9 695.4 %reduce-scatter.30.cloned.1.call-start = ((), (), s32[]{:S(2)}) async-start(), calls=%async_computation.22 | async-start | bytes 5013504 | tf_op jit(solution)/shard_map/reduce_scatter | solution.py:307
  821.9 745.9 %reduce-scatter.18.cloned.1.call-start = ((), (), s32[]{:S(2)}) async-start(), calls=%async_computation.16 | async-start | bytes 1253376 | tf_op jit(solution)/shard_map/reduce_scatter | solution.py:289
  1159.2 10.5 slice-start.2
  1161.4 4.1 copy-start.79
  1161.4 4.1 copy-start.67
  1161.4 8.3 slice-start.3
  1161.4 8.3 slice-start.4
  1169.7 8.3 copy-start.71
  1169.7 8.3 copy-start.81
  1181.2 457.6 %reduce-scatter.22.cloned.1.call-start = ((), (), s32[]{:S(2)}) async-start(), calls=%async_computation.18 | async-start | bytes 3760128 | tf_op jit(solution)/shard_map/reduce_scatter | solution.py:295
  1198.6 563.8 %reduce-scatter.20.cloned.1.call-start = ((), (), s32[]{:S(2)}) async-start(), calls=%async_computation.17 | async-start | bytes 11280384 | tf_op jit(solution)/shard_map/reduce_scatter | solution.py:292
  1217.9 544.5 %copy-start.82 = (f32[64,16]{1,0:T(8,128)S(1)}, f32[64,16]{1,0:T(8,128)}, u32[]{:S(2)}) copy-start(f32[64,16]{1,0:T(8,128)} %get-tuple-element.14) | copy-start | bytes 12292
  1218.0 604.2 %reduce-scatter.16.cloned.1.call-start = ((), (), s32[]{:S(2)}) async-start(), calls=%async_computation.15 | async-start | bytes 417792 | tf_op jit(solution)/shard_map/reduce_scatter | solution.py:286
  1221.9 661.0 %all-reduce.3.cloned.1.call-start = ((), (), s32[]{:S(2)}) async-start(), calls=%async_computation.24 | async-start | bytes 3833856 | tf_op jit(solution)/shard_map/psum | solution.py:316
  1762.5 133.4 %copy-start.1 = (bf16[768,2304]{1,0:T(8,128)(2,1)S(1)}, bf16[768,2304]{1,0:T(8,128)(2,1)}, u32[]{:S(2)}) copy-start(bf16[768,2304]{1,0:T(8,128)(2,1)} %param.21) | copy-start | bytes 10616836
  1882.9 11.8 copy-start.65
  (49 other events, 105.8 us)
Sparse Core Ops, SparseCore 0:
  62.2 131.2 all-gather.4
  195.6 128.5 all-gather.2
  667.1 243.2 reduce-scatter.13
  914.3 242.3 reduce-scatter.11
  1160.2 57.2 reduce-scatter.27
  1221.0 57.1 reduce-scatter.23
  1282.1 67.1 reduce-scatter.25
  1353.1 74.5 reduce-scatter.31
  1431.5 74.7 reduce-scatter.29
  1510.3 57.4 reduce-scatter.17
  1571.7 67.1 reduce-scatter.21
  1642.7 119.6 reduce-scatter.19
  1766.5 55.6 reduce-scatter.15
  1824.7 58.1 all-reduce.2
where the time goes:
time: 1920 us; the launch traced here: 1900 us
  waiting for transfers between devices  1150 us (60%)
  local copies, waits for them, and re-layouts  321 us (17%)
  matrix products  304 us (16%)
  other arithmetic  97.4 us (5%)
    reduce_scatter x1, waiting for transfers between devices, on_device(): lax.psum_scatter(key_terms.reshape(frames, patch_count, model_width).asty...  246 us
    all_gather x1, waiting for transfers between devices, on_device(): lax.all_gather(k_local, 'pos', axis=1, tiled=True)  125 us
    reduce_scatter x1, waiting for transfers between devices, on_device(): lax.psum_scatter(grad_adaln_weight.astype(jnp.bfloat16), 'pos', scatter_d...  124 us
    reduce_scatter x1, waiting for transfers between devices, on_device(): lax.psum_scatter(grad_hidden_up.astype(jnp.bfloat16), 'pos', scatter_dime...  78.6 us
    reduce_scatter x1, waiting for transfers between devices, on_device(): lax.psum_scatter(grad_hidden_down.astype(jnp.bfloat16), 'pos', scatter_di...  78.5 us
    all_gather x1, waiting for transfers between devices, on_device(): lax.all_gather(v_local, 'pos', axis=1, tiled=True)  71.5 us
    reduce_scatter x1, waiting for transfers between devices, on_device(): lax.psum_scatter(grad_spatial_in.astype(jnp.bfloat16), 'pos', scatter_dim...  71 us
    reduce_scatter x1, waiting for transfers between devices, on_device(): lax.psum_scatter(grad_temporal_in.astype(jnp.bfloat16), 'pos', scatter_di...  71 us
  transfers between devices with their start and end apart: 14, of which 13 were waited for; matrix products, arithmetic and copies ran while one was open for 16% of the time, Pallas kernels for 0%

commit v1 on v0

--- a/solution.py
+++ b/solution.py
@@ -11,6 +11,18 @@
 epsilon = 1e-06
 highest = lax.Precision.HIGHEST
 masked_score = -1000000000.0
+
+
+def collect(x, axis, dim):
+    ways, here, hop = (lax.axis_size(axis), lax.axis_index(axis), x.shape[dim])
+    line, have = (x, 1)
+    while have < ways:
+        line = jnp.concatenate(
+            [line, lax.ppermute(line, axis, [(d, (d - have) % ways) for d in range(ways)])],
+            axis=dim,
+        )
+        have = 2 * have
+    return jnp.roll(line, here * hop, axis=dim)
 
 
 def frequency(step_ids):
@@ -114,10 +126,7 @@
     q_space = qkv_one[:, :, 0]
     k_local = qkv_one[:, :, 1].reshape(frames, places, model_width)
     v_local = qkv_one[:, :, 2].reshape(frames, places, model_width)
-    k_all, v_all = (
-        lax.all_gather(k_local, "pos", axis=1, tiled=True),
-        lax.all_gather(v_local, "pos", axis=1, tiled=True),
-    )
+    k_all, v_all = (collect(k_local, "pos", 1), lax.all_gather(v_local, "pos", axis=1, tiled=True))
     patch_count = k_all.shape[1]
     k_heads = k_all.reshape(frames, patch_count, HEADS, HEAD_DIM)
     v_heads = v_all.reshape(frames, patch_count, HEADS, HEAD_DIM)

time: 1920 us -> 2680 us (1.40)
  waiting for transfers between devices: 1150 us -> 1850 us
  local copies, waits for them, and re-layouts: 321 us -> 384 us
    ppermute x0 -> x4, waiting for transfers between devices: none -> 862 us  [collect(): lax.ppermute(line, axis, [(d, (d - have) % ways) for d in range(ways)])]
    reduce_scatter x1, waiting for transfers between devices: 66.5 us -> 247 us  [on_device(): lax.psum_scatter(value_terms.reshape(frames, patch_count, model_width).as...]
    reduce_scatter x1, waiting for transfers between devices: 246 us -> 97 us  [on_device(): lax.psum_scatter(key_terms.reshape(frames, patch_count, model_width).asty...]
    all_gather x1 -> x0, waiting for transfers between devices: 125 us -> none  [on_device(): lax.all_gather(k_local, 'pos', axis=1, tiled=True)]
    all_gather x1, waiting for transfers between devices: 71.5 us -> 0.01 us  [on_device(): lax.all_gather(v_local, 'pos', axis=1, tiled=True)]
    dynamic_slice x0 -> x2, local copies, waits for them, and re-layouts: none -> 51 us  [collect(): return jnp.roll(line, here * hop, axis=dim)]
    all_gather x1 -> x0, local copies, waits for them, and re-layouts: 30.7 us -> none  [on_device(): lax.all_gather(k_local, 'pos', axis=1, tiled=True)]
    unnamed x208 -> x235, local copies, waits for them, and re-layouts: 27.5 us -> 58 us
  transfers between devices with their start and end apart: 14 -> 17, of which waited for: 13 -> 15; matrix products, arithmetic and copies ran while one was open for 16% -> 13% of each run, Pallas kernels for 0% -> 0%
where the time goes in v1:
time: 2680 us; the launch traced here: 2670 us
  waiting for transfers between devices  1850 us (69%)
  local copies, waits for them, and re-layouts  384 us (14%)
  matrix products  299 us (11%)
  other arithmetic  99.3 us (4%)
    ppermute x4, waiting for transfers between devices, collect(): lax.ppermute(line, axis, [(d, (d - have) % ways) for d in range(ways)])  862 us
    reduce_scatter x1, waiting for transfers between devices, on_device(): lax.psum_scatter(value_terms.reshape(frames, patch_count, model_width).as...  247 us
    reduce_scatter x1, waiting for transfers between devices, on_device(): lax.psum_scatter(grad_adaln_weight.astype(jnp.bfloat16), 'pos', scatter_d...  124 us
    reduce_scatter x1, waiting for transfers between devices, on_device(): lax.psum_scatter(key_terms.reshape(frames, patch_count, model_width).asty...  97 us
    reduce_scatter x1, waiting for transfers between devices, on_device(): lax.psum_scatter(grad_hidden_down.astype(jnp.bfloat16), 'pos', scatter_di...  78.7 us
    reduce_scatter x1, waiting for transfers between devices, on_device(): lax.psum_scatter(grad_hidden_up.astype(jnp.bfloat16), 'pos', scatter_dime...  78.3 us
    reduce_scatter x1, waiting for transfers between devices, on_device(): lax.psum_scatter(grad_temporal_in.astype(jnp.bfloat16), 'pos', scatter_di...  70.9 us
    reduce_scatter x1, waiting for transfers between devices, on_device(): lax.psum_scatter(grad_spatial_in.astype(jnp.bfloat16), 'pos', scatter_dim...  70.9 us
  transfers between devices with their start and end apart: 17, of which 15 were waited for; matrix products, arithmetic and copies ran while one was open for 13% of the time, Pallas kernels for 0%

profile of v1, /device:TPU:0, one launch (start us, length us, event | category | flops | bytes accessed | tf_op | source)
XLA Modules:
  0.0 2665.9 jit_solution(15501055001087952348)
XLA Ops:
  13.0 7.0 fusion.78
  32.2 15.0 reshape.275
  47.1 9.3 fusion.90
  56.4 6.1 reshape_squeeze.6
  62.6 6.1 reshape_squeeze.7
  68.7 5.4 collective-permute-start
  74.1 52.1 %collective-permute-done = bf16[64,16,768]{2,1,0:T(8,128)(2,1)S(1)} collective-permute-done((bf16[64,16,768]{2,1,0:T(8,128)(2,1)}, bf16[64,16,768]{2,1,0:T(8,128)(2,1)S(1)}, u32[]{:S(2)}, u32[]{:S(2)}) %collective-permute-start) | collective-permute-done | bytes 1572896 | tf_op jit(solution)/shard_map/ppermute | solution.py:21
  128.8 137.3 %collective-permute-done.1 = bf16[64,32,768]{2,1,0:T(8,128)(2,1)S(1)} collective-permute-done((bf16[64,32,768]{2,1,0:T(8,128)(2,1)S(1)}, bf16[64,32,768]{2,1,0:T(8,128)(2,1)S(1)}, u32[]{:S(2)}, u32[]{:S(2)}) %collective-permute-start.1) | collective-permute-done | bytes 3145760 | tf_op jit(solution)/shard_map/ppermute | solution.py:21
  267.4 143.5 %collective-permute-done.2 = bf16[64,64,768]{2,1,0:T(8,128)(2,1)S(1)} collective-permute-done((bf16[64,64,768]{2,1,0:T(8,128)(2,1)S(1)}, bf16[64,64,768]{2,1,0:T(8,128)(2,1)S(1)}, u32[]{:S(2)}, u32[]{:S(2)}) %collective-permute-start.2) | collective-permute-done | bytes 6291488 | tf_op jit(solution)/shard_map/ppermute | solution.py:21
  411.0 6.5 pad_maximum_fusion
  431.9 528.7 %collective-permute-done.3 = bf16[64,128,768]{2,1,0:T(8,128)(2,1)} collective-permute-done((bf16[64,128,768]{2,1,0:T(8,128)(2,1)}, bf16[64,128,768]{2,1,0:T(8,128)(2,1)}, u32[]{:S(2)}, u32[]{:S(2)}) %collective-permute-start.3) | collective-permute-done | bytes 12582944 | tf_op jit(solution)/shard_map/ppermute | solution.py:21
  960.6 10.9 constant_dynamic-update-slice_fusion.5
  979.1 10.8 constant_dynamic-update-slice_fusion
  989.9 21.0 constant_dynamic-slice_fusion
  1010.9 30.0 %copy.84 = bf16[64,256,768]{1,2,0:T(8,128)(2,1)} copy(bf16[64,256,768]{2,1,0:T(8,128)(2,1)} %constant_dynamic-slice_fusion) | data formatting | bytes 50331648 | tf_op jit(solution)/shard_map/jit(_roll_dynamic)/dynamic_slice | solution.py:25
  1040.9 18.4 multiply_reduce_fusion.1
  1059.2 8.6 exponential_reduce_fusion
  1068.7 32.6 %copy.82 = bf16[64,256,768]{1,2,0:T(8,128)(2,1)} copy(bf16[64,256,768]{2,1,0:T(8,128)(2,1)} %all-gather.2.cloned.1.call-done) | data formatting | bytes 50331648 | tf_op jit(solution)/shard_map/all_gather | solution.py:129
  1101.3 16.2 convert_bitcast_fusion
  1122.5 6.5 dot_general.132
  1142.9 15.0 reshape.279
  1157.9 7.7 fusion.89
  1173.8 6.6 copy.124
  1180.3 6.8 fusion.32
  1192.1 5.9 fusion.87
  1200.9 7.0 fusion.93
  1207.9 7.3 fusion.86
  1215.3 16.5 fusion.6
  1231.7 8.6 fusion.94
  1256.3 5.9 reshape.285
  1262.2 6.5 copy.99
  1268.8 7.2 multiply_reduce_fusion.2
  1280.6 7.4 multiply_bitcast_fusion.2
  1296.6 9.7 maximum_convert_fusion
  1306.2 12.3 copy.102
  1318.5 15.7 convert_element_type.240
  1334.4 7.5 multiply_reduce_fusion.6
  1357.5 20.3 multiply_reduce_fusion
  1377.8 10.3 multiply_convert_fusion.1
  1388.1 13.8 multiply_convert_fusion
  1402.0 32.9 %copy.105 = bf16[64,256,768]{2,1,0:T(8,128)(2,1)} copy(bf16[64,256,768]{1,2,0:T(8,128)(2,1)} %bitcast.162) | data formatting | bytes 50331648 | tf_op jit(solution)/shard_map/convert_element_type | solution.py:256
  1434.9 20.2 convolution_convert_fusion
  1455.1 31.3 %copy.107 = bf16[64,256,768]{2,1,0:T(8,128)(2,1)} copy(bf16[64,256,768]{1,2,0:T(8,128)(2,1)} %bitcast.161) | data formatting | bytes 50331648 | tf_op jit(solution)/shard_map/convert_element_type | solution.py:262
  1488.3 6.0 copy.112
  1510.2 15.9 convert_element_type.264
  1526.1 7.7 convolution_convert_fusion.6
  1535.3 9.8 convolution_convert_fusion.5
  1546.5 11.6 convolution_convert_fusion.4
  1558.2 13.4 multiply_bitcast_fusion
  1580.1 97.0 %reduce-scatter.12.cloned.1.call-done = bf16[64,16,768]{2,1,0:T(8,128)(2,1)} async-done(((bf16[64,256,768]{2,1,0:T(8,128)(2,1)}), bf16[64,16,768]{2,1,0:T(8,128)(2,1)}) %reduce-scatter.12.cloned.1.call-update) | async-done | bytes 1572880 | tf_op jit(solution)/shard_map/reduce_scatter | solution.py:255
  1677.1 246.5 %reduce-scatter.14.cloned.1.call-done = bf16[64,16,768]{2,1,0:T(8,128)(2,1)} async-done(((bf16[64,256,768]{2,1,0:T(8,128)(2,1)}), bf16[64,16,768]{2,1,0:T(8,128)(2,1)}) %reduce-scatter.14.cloned.1.call-update) | async-done | bytes 1572880 | tf_op jit(solution)/shard_map/reduce_scatter | solution.py:261
  1936.6 8.3 fusion.95
  1952.0 6.5 copy.108
  1965.4 19.3 convolution_convert_fusion.1
  1988.7 56.4 %reduce-scatter.24.cloned.1.call-done = bf16[48,768]{1,0:T(8,128)(2,1)} async-done(((bf16[768,768]{1,0:T(8,128)(2,1)}), bf16[48,768]{1,0:T(8,128)(2,1)}) %reduce-scatter.24.cloned.1.call-update) | async-done | bytes 73744 | tf_op jit(solution)/shard_map/reduce_scatter | solution.py:307
  2045.1 70.9 %reduce-scatter.26.cloned.1.call-done = bf16[48,2304]{1,0:T(8,128)(2,1)} async-done(((bf16[768,2304]{1,0:T(8,128)(2,1)}), bf16[48,2304]{1,0:T(8,128)(2,1)}) %reduce-scatter.26.cloned.1.call-update) | async-done | bytes 221200 | tf_op jit(solution)/shard_map/reduce_scatter | solution.py:310
  2116.1 78.3 %reduce-scatter.30.cloned.1.call-done = bf16[48,3072]{1,0:T(8,128)(2,1)} async-done(((bf16[768,3072]{1,0:T(8,128)(2,1)}), bf16[48,3072]{1,0:T(8,128)(2,1)}) %reduce-scatter.30.cloned.1.call-update) | async-done | bytes 294928 | tf_op jit(solution)/shard_map/reduce_scatter | solution.py:316
  2194.3 78.7 %reduce-scatter.32.cloned.1.call-done = bf16[192,768]{1,0:T(8,128)(2,1)} async-done(((bf16[3072,768]{1,0:T(8,128)(2,1)}), bf16[192,768]{1,0:T(8,128)(2,1)}) %reduce-scatter.32.cloned.1.call-update) | async-done | bytes 294928 | tf_op jit(solution)/shard_map/reduce_scatter | solution.py:319
  2273.0 61.7 %reduce-scatter.18.cloned.1.call-done = bf16[48,768]{1,0:T(8,128)(2,1)} async-done(((bf16[768,768]{1,0:T(8,128)(2,1)}), bf16[48,768]{1,0:T(8,128)(2,1)}) %reduce-scatter.18.cloned.1.call-update) | async-done | bytes 73744 | tf_op jit(solution)/shard_map/reduce_scatter | solution.py:298
  2334.6 70.9 %reduce-scatter.22.cloned.1.call-done = bf16[48,2304]{1,0:T(8,128)(2,1)} async-done(((bf16[768,2304]{1,0:T(8,128)(2,1)}), bf16[48,2304]{1,0:T(8,128)(2,1)}) %reduce-scatter.22.cloned.1.call-update) | async-done | bytes 221200 | tf_op jit(solution)/shard_map/reduce_scatter | solution.py:304
  2405.5 123.6 %reduce-scatter.20.cloned.1.call-done = bf16[48,6912]{1,0:T(8,128)(2,1)} async-done(((bf16[768,6912]{1,0:T(8,128)(2,1)}), bf16[48,6912]{1,0:T(8,128)(2,1)}) %reduce-scatter.20.cloned.1.call-update) | async-done | bytes 663568 | tf_op jit(solution)/shard_map/reduce_scatter | solution.py:301
  2534.2 54.5 %reduce-scatter.16.cloned.1.call-done = bf16[16,768]{1,0:T(8,128)(2,1)} async-done(((bf16[256,768]{1,0:T(8,128)(2,1)}), bf16[16,768]{1,0:T(8,128)(2,1)}) %reduce-scatter.16.cloned.1.call-update) | async-done | bytes 24592 | tf_op jit(solution)/shard_map/reduce_scatter | solution.py:295
  2588.7 9.5 psum.63
  2599.6 50.0 %all-reduce.3.cloned.1.call-done = (bf16[48,768]{1,0:T(8,128)(2,1)}, bf16[48,6912]{1,0:T(8,128)(2,1)}, bf16[48,2304]{1,0:T(8,128)(2,1)}, bf16[48,768]{1,0:T(8,12...) async-done(((bf16[48,768]{1,0:T(8,128)(2,1)}, bf16[48,6912]{1,0:T(8,128)(2,1)}, ...) | async-done | bytes 1916944 | tf_op jit(solution)/shard_map/psum | solution.py:325
  (348 shorter events, 199.8 us)
Async XLA Ops:
  7.2 1130.3 %copy-start = (bf16[768,2304]{1,0:T(8,128)(2,1)S(1)}, bf16[768,2304]{1,0:T(8,128)(2,1)}, u32[]{:S(2)}) copy-start(bf16[768,2304]{1,0:T(8,128)(2,1)} %param.21) | copy-start | bytes 10616836
  7.2 1061.5 %all-gather.2.cloned.1.call-start = ((), (), s32[]{:S(2)}) async-start(), calls=%async_computation.11 | async-start | bytes 26738688 | tf_op jit(solution)/shard_map/all_gather | solution.py:129
  9.2 412.9 %copy-start.94 = (s32[64]{0:T(128)}, s32[64]{0:T(128)S(1)}, u32[]{:S(2)}) copy-start(s32[64]{0:T(128)S(1)} %convert_reduce_fusion.1) | copy-start | bytes 772
  13.0 7.0 copy-start.73
  62.5 1614.5 %reduce-scatter.12.cloned.1.call-start = ((), (), s32[]{:S(2)}) async-start(), calls=%async_computation.12 | async-start | bytes 26738688 | tf_op jit(solution)/shard_map/reduce_scatter | solution.py:255
  68.7 197.5 %copy-start.6 = (bf16[64,16,768]{2,1,0:T(8,128)(2,1)S(1)}, bf16[64,16,768]{2,1,0:T(8,128)(2,1)}, u32[]{:S(2)}) copy-start(bf16[64,16,768]{2,1,0:T(8,128)(2,1)} %reshape_squeeze.7) | copy-start | bytes 4718596
  68.7 57.5 %collective-permute-start = (bf16[64,16,768]{2,1,0:T(8,128)(2,1)}, bf16[64,16,768]{2,1,0:T(8,128)(2,1)S(1)}, u32[]{:S(2)}, u32[]{:S(2)}) collective-permute-start(bf16[64,16,768]{2,1,0:T(8,128)(2,1)} %reshape_squeeze.7), channel_id=1, source_target_pairs={{0,15},{1,0},{2,1},{3,2},{4,3},{5,4},{6,5},{7,6},{8,7},{9,8},{10,9... | collective-permute-start | bytes 4718600 | tf_op jit(solution)/shard_map/ppermute | solution.py:21
  126.2 284.7 %copy-start.14 = (bf16[64,16,768]{2,1,0:T(8,128)(2,1)}, bf16[64,16,768]{2,1,0:T(8,128)(2,1)S(1)}, u32[]{:S(2)}) copy-start(bf16[64,16,768]{2,1,0:T(8,128)(2,1)S(1)} %collective-permute-done) | copy-start | bytes 4718596
  128.6 137.5 %collective-permute-start.1 = (bf16[64,32,768]{2,1,0:T(8,128)(2,1)S(1)}, bf16[64,32,768]{2,1,0:T(8,128)(2,1)S(1)}, u32[]{:S(2)}, u32[]{:S(2)}) collective-permute-start(bf16[64,32,768]{2,1,0:T(8,128)(2,1)S(1)} %pad_maximum_fusion.2), channel_id=1, source_target_pairs={{0,14},{1,15},{2,0},{3,1},{4,2},{5,3},{6,4},{7,5},{8,6},{9,7},{10,... | collective-permute-start | bytes 9437192 | tf_op jit(solution)/shard_map/ppermute | solution.py:21
  266.2 144.8 %copy-start.11 = (bf16[64,32,768]{2,1,0:T(8,128)(2,1)}, bf16[64,32,768]{2,1,0:T(8,128)(2,1)S(1)}, u32[]{:S(2)}) copy-start(bf16[64,32,768]{2,1,0:T(8,128)(2,1)S(1)} %collective-permute-done.1) | copy-start | bytes 9437188
  266.9 144.0 %collective-permute-start.2 = (bf16[64,64,768]{2,1,0:T(8,128)(2,1)S(1)}, bf16[64,64,768]{2,1,0:T(8,128)(2,1)S(1)}, u32[]{:S(2)}, u32[]{:S(2)}) collective-permute-start(bf16[64,64,768]{2,1,0:T(8,128)(2,1)S(1)} %pad_maximum_fusion.1), channel_id=1, source_target_pairs={{0,12},{1,13},{2,14},{3,15},{4,0},{5,1},{6,2},{7,3},{8,4},{9,5},{1... | collective-permute-start | bytes 18874376 | tf_op jit(solution)/shard_map/ppermute | solution.py:21
  410.9 6.5 copy-start.8
  417.4 543.2 %collective-permute-start.3 = (bf16[64,128,768]{2,1,0:T(8,128)(2,1)}, bf16[64,128,768]{2,1,0:T(8,128)(2,1)}, u32[]{:S(2)}, u32[]{:S(2)}) collective-permute-start(bf16[64,128,768]{2,1,0:T(8,128)(2,1)} %pad_maximum_fusion), channel_id=1, source_target_pairs={{0,8},{1,9},{2,10},{3,11},{4,12},{5,13},{6,14},{7,15},{8,0},{9,1},... | collective-permute-start | bytes 37748744 | tf_op jit(solution)/shard_map/ppermute | solution.py:21
  419.2 9.6 slice-start.5
  422.1 6.7 slice-start.6
  431.9 539.6 %copy-start.7 = (bf16[64,16,768]{2,1,0:T(8,128)(2,1)S(1)}, bf16[64,16,768]{2,1,0:T(8,128)(2,1)}, u32[]{:S(2)}) copy-start(bf16[64,16,768]{2,1,0:T(8,128)(2,1)} %reshape_squeeze.7) | copy-start | bytes 4718596
  960.6 12.2 copy-start.15
  1059.2 8.6 copy-start.31
  1198.0 9.8 slice-start.7
  1200.9 7.0 slice-start.8
  1207.9 7.4 copy-start.98
  1207.9 7.4 copy-start.44
  1215.2 27.9 %copy-start.25 = (f32[1024,768]{1,0:T(8,128)}, f32[1024,768]{1,0:T(8,128)S(1)}, u32[]{:S(2)}) copy-start(f32[1024,768]{1,0:T(8,128)S(1)} %fusion.86) | copy-start | bytes 9437188
  1268.8 7.2 copy-start.33
  1280.6 7.4 copy-start.23
  1280.6 12.6 slice-start
  1288.0 5.2 slice-start.1
  1288.0 5.2 copy-start.18
  1334.3 7.6 copy-start.79
  1334.3 7.6 copy-start.4
  1334.3 7.6 copy-start.35
  1334.3 7.6 copy-start.57
  1334.3 7.6 copy-start.72
  1334.3 10.5 copy-start.26
  1334.3 10.5 copy-start.27
  1334.3 10.5 copy-start.28
  1344.9 5.8 copy-start.41
  1388.1 13.8 copy-start.5
  1434.8 488.8 %reduce-scatter.14.cloned.1.call-start = ((), (), s32[]{:S(2)}) async-start(), calls=%async_computation.13 | async-start | bytes 26738688 | tf_op jit(solution)/shard_map/reduce_scatter | solution.py:261
  1486.5 502.2 %reduce-scatter.28.cloned.1.call-start = ((), (), s32[]{:S(2)}) async-start(), calls=%async_computation.20 | async-start | bytes 1253376 | tf_op jit(solution)/shard_map/reduce_scatter | solution.py:313
  1494.3 5.4 copy-start.51
  1502.2 5.4 copy-start.53
  1502.2 542.9 %reduce-scatter.24.cloned.1.call-start = ((), (), s32[]{:S(2)}) async-start(), calls=%async_computation.18 | async-start | bytes 1253376 | tf_op jit(solution)/shard_map/reduce_scatter | solution.py:307
  1510.1 16.0 copy-start.47
  1510.1 605.9 %reduce-scatter.26.cloned.1.call-start = ((), (), s32[]{:S(2)}) async-start(), calls=%async_computation.19 | async-start | bytes 3760128 | tf_op jit(solution)/shard_map/reduce_scatter | solution.py:310
  1533.9 660.5 %reduce-scatter.30.cloned.1.call-start = ((), (), s32[]{:S(2)}) async-start(), calls=%async_computation.21 | async-start | bytes 5013504 | tf_op jit(solution)/shard_map/reduce_scatter | solution.py:316
  1545.1 727.9 %reduce-scatter.32.cloned.1.call-start = ((), (), s32[]{:S(2)}) async-start(), calls=%async_computation.22 | async-start | bytes 5013504 | tf_op jit(solution)/shard_map/reduce_scatter | solution.py:319
  1558.2 776.5 %reduce-scatter.18.cloned.1.call-start = ((), (), s32[]{:S(2)}) async-start(), calls=%async_computation.15 | async-start | bytes 1253376 | tf_op jit(solution)/shard_map/reduce_scatter | solution.py:298
  1926.1 10.5 slice-start.2
  1928.3 8.3 slice-start.3
  1928.3 8.3 slice-start.4
  1936.6 8.3 copy-start.74
  1936.6 8.3 copy-start.85
  1948.1 457.4 %reduce-scatter.22.cloned.1.call-start = ((), (), s32[]{:S(2)}) async-start(), calls=%async_computation.17 | async-start | bytes 3760128 | tf_op jit(solution)/shard_map/reduce_scatter | solution.py:304
  1965.4 563.8 %reduce-scatter.20.cloned.1.call-start = ((), (), s32[]{:S(2)}) async-start(), calls=%async_computation.16 | async-start | bytes 11280384 | tf_op jit(solution)/shard_map/reduce_scatter | solution.py:301
  1984.7 544.5 %copy-start.86 = (f32[64,16]{1,0:T(8,128)S(1)}, f32[64,16]{1,0:T(8,128)}, u32[]{:S(2)}) copy-start(f32[64,16]{1,0:T(8,128)} %get-tuple-element.14) | copy-start | bytes 12292
  1984.7 604.0 %reduce-scatter.16.cloned.1.call-start = ((), (), s32[]{:S(2)}) async-start(), calls=%async_computation.14 | async-start | bytes 417792 | tf_op jit(solution)/shard_map/reduce_scatter | solution.py:295
  1988.6 660.9 %all-reduce.3.cloned.1.call-start = ((), (), s32[]{:S(2)}) async-start(), calls=%async_computation.23 | async-start | bytes 3833856 | tf_op jit(solution)/shard_map/psum | solution.py:325
  2529.2 129.9 %copy-start.1 = (bf16[768,2304]{1,0:T(8,128)(2,1)S(1)}, bf16[768,2304]{1,0:T(8,128)(2,1)}, u32[]{:S(2)}) copy-start(bf16[768,2304]{1,0:T(8,128)(2,1)} %param.21) | copy-start | bytes 10616836
  2649.6 6.0 copy-start.83
  2649.6 6.7 copy-start.82
  2649.6 7.5 copy-start.89
  2649.6 8.2 copy-start.88
  2649.6 8.9 copy-start.87
  (61 other events, 146.2 us)
Sparse Core Ops, SparseCore 0:
  62.7 221.0 all-gather.1
  1435.0 242.0 reduce-scatter.11
  1681.2 242.3 reduce-scatter.13
  1927.1 57.2 reduce-scatter.27
  1987.9 57.2 reduce-scatter.23
  2048.9 67.1 reduce-scatter.25
  2119.9 74.3 reduce-scatter.29
  2198.2 74.7 reduce-scatter.31
  2277.2 57.4 reduce-scatter.17
  2338.4 67.1 reduce-scatter.21
  2409.6 119.5 reduce-scatter.19
  2533.1 55.6 reduce-scatter.15
  2591.4 58.1 all-reduce.2
